TPU v7x, 32 devices: a whole 2x2x4 slice. The times are simulated.
32 devices in a mesh: section: 2 (over x), seq: 4 (over z), tensor: 4 (over y, core).
Axes of the slice: x: 2, y: 2, z: 4, core: 2. Of those that a mesh axis runs over, the one named last changes fastest.
Arguments:
- q_mant: bfloat16 [2, 256, 16384], P('section', 'seq', 'tensor'), may hold values from -32 to 32
- q_scale: int32 [2, 256, 512], P('section', 'seq', 'tensor'), may hold values from -2 to 2
- key_mantissa_block: bfloat16 [2, 256, 1024], P('section', 'seq', 'tensor'), may hold values from -32 to 32
- key_exponent_scale: int32 [2, 256, 32], P('section', 'seq', 'tensor'), may hold values from -2 to 2
- value_mantissa_block: bfloat16 [2, 256, 1024], P('section', 'seq', 'tensor'), may hold values from -6 to 6
- value_exponent_scale: int32 [2, 256, 32], P('section', 'seq', 'tensor'), may hold values from -1 to 1
- cached_key_rows: bfloat16 [2, 8, 512, 128], P('section', 'tensor', 'seq'), may hold values from -12 to 12
- cached_value_rows: bfloat16 [2, 8, 512, 128], P('section', 'tensor', 'seq'), may hold values from -8 to 8
- start: int32 [2], P('section'), may hold values from 256 to 512, as said below
Outputs:
- attended: bfloat16 [2, 256, 16384], P('section', 'seq', 'tensor')
Inputs may be any that keep to these rules, and one draw needn't show every extreme that they name: The first start[s] cached positions of section s hold earlier tokens; the cache of some section is full in every draw.
All inputs are finite; a program needn't handle non-finite values.
Results may differ from a plain program's by a relative error of at most 0.0023.
Values may be sent and summed in bfloat16 or wider, within the bound.
No kernel may reach another device: no remote copies, remote signals or barrier semaphores. Data moves between devices by JAX's collectives and lax.ppermute only.
A program may use at most 64 MiB of HBM per device.

v0:
```python
import math
import jax
import jax.numpy as jnp
from jax import lax
from jax.sharding import PartitionSpec as P


def shifted(block, axis, distance):
    devices = range(lax.axis_size(axis))
    route = [((i - distance) % len(devices), i) for i in devices]
    return lax.ppermute(block, axis, route)


def decode_mantissas(mantissa, exponent):
    row_count, feature_count = mantissa.shape
    blocks = mantissa.astype(jnp.float32).reshape(row_count, feature_count // 32, 32)
    factor = jnp.exp2(exponent.astype(jnp.float32))[:, :, None]
    return (blocks * factor).reshape(row_count, feature_count).astype(jnp.bfloat16)


def attend(running, queries, section_key_rows, section_value_rows, key_start, from_cache, limit):
    head_count, tokens, head_size = queries.shape
    key_count = section_key_rows.shape[1]
    block_rows = min(512, tokens)
    inv_root = 1.0 / math.sqrt(head_size)
    key_first = jnp.asarray(key_start, jnp.int32)
    key_index = lax.iota(jnp.int32, key_count)

    def one_block(number, running):
        first_row = number * block_rows

        def update(running):
            row_max, row_total, row_sum = running
            query_block = lax.dynamic_slice_in_dim(queries, first_row, block_rows, 1)
            scores = (
                jnp.einsum(
                    "hqd,hkd->hqk",
                    query_block,
                    section_key_rows,
                    preferred_element_type=jnp.float32,
                )
                * inv_root
            )
            if from_cache:
                allowed = jnp.broadcast_to((key_index < limit)[None, None, :], scores.shape)
            else:
                query_index = first_row + lax.iota(jnp.int32, block_rows)
                allowed = jnp.broadcast_to(
                    (key_index[None, :] <= query_index[:, None])[None], scores.shape
                )
            scores = jnp.where(allowed, scores, -1e30)
            old_max = lax.dynamic_slice_in_dim(row_max, first_row, block_rows, 1)
            new_max = jnp.maximum(old_max, jnp.max(scores, axis=2))
            weights = jnp.where(allowed, jnp.exp(scores - new_max[:, :, None]), 0.0)
            factor = jnp.exp(old_max - new_max)
            old_total = lax.dynamic_slice_in_dim(row_total, first_row, block_rows, 1)
            new_total = old_total * factor + jnp.sum(weights, axis=2)
            product = jnp.einsum(
                "hqk,hkd->hqd",
                weights.astype(jnp.bfloat16),
                section_value_rows,
                preferred_element_type=jnp.float32,
            )
            old_sum = lax.dynamic_slice_in_dim(row_sum, first_row, block_rows, 1)
            new_sum = old_sum * factor[:, :, None] + product
            return (
                lax.dynamic_update_slice_in_dim(row_max, new_max, first_row, 1),
                lax.dynamic_update_slice_in_dim(row_total, new_total, first_row, 1),
                lax.dynamic_update_slice_in_dim(row_sum, new_sum, first_row, 1),
            )

        if from_cache:
            visible = key_first < limit
        else:
            visible = key_first <= first_row + block_rows - 1
        return lax.cond(visible, update, lambda unchanged: unchanged, running)

    return lax.fori_loop(0, tokens // block_rows, one_block, running)


def body(
    q_mant,
    q_scale,
    key_mantissa_block,
    key_exponent_scale,
    value_mantissa_block,
    value_exponent_scale,
    cached_key_rows,
    cached_value_rows,
    start,
):
    arrived = shifted(
        (
            q_mant[0],
            key_mantissa_block[0],
            value_mantissa_block[0],
            q_scale[0].astype(jnp.bfloat16),
            key_exponent_scale[0].astype(jnp.bfloat16),
            value_exponent_scale[0].astype(jnp.bfloat16),
        ),
        "section",
        1,
    )
    row_count = q_mant.shape[1]
    kv_here = cached_key_rows.shape[1]
    head_size = cached_key_rows.shape[3]
    queries = decode_mantissas(arrived[0], arrived[3]).reshape(row_count, -1, head_size)
    section_key_rows = decode_mantissas(arrived[1], arrived[4]).reshape(
        row_count, kv_here, head_size
    )
    section_value_rows = decode_mantissas(arrived[2], arrived[5]).reshape(
        row_count, kv_here, head_size
    )
    heads_here = queries.shape[1]
    query_group_width = heads_here // kv_here
    seq_count = lax.axis_size("seq")
    local_heads = heads_here // seq_count
    tokens = row_count * seq_count
    limit = start[0]
    mine = lax.all_to_all(queries, "seq", split_axis=1, concat_axis=0, tiled=True)
    query_block = jnp.transpose(mine, (1, 0, 2))
    running = (
        jnp.full((local_heads, tokens), -1e30, jnp.float32),
        jnp.zeros((local_heads, tokens), jnp.float32),
        jnp.zeros((local_heads, tokens, head_size), jnp.float32),
    )
    head_ids = lax.axis_index("seq") * local_heads + lax.iota(jnp.int32, local_heads)
    kv_ids = head_ids // query_group_width
    pieces = (
        lax.all_gather(cached_key_rows[0], "seq", axis=1, tiled=True),
        lax.all_gather(cached_value_rows[0], "seq", axis=1, tiled=True),
    )
    running = attend(
        running,
        query_block,
        jnp.take(pieces[0], kv_ids, axis=0),
        jnp.take(pieces[1], kv_ids, axis=0),
        jnp.int32(0),
        True,
        limit,
    )
    pieces = (
        lax.all_gather(section_key_rows, "seq", axis=0, tiled=True),
        lax.all_gather(section_value_rows, "seq", axis=0, tiled=True),
    )
    picked_keys = jnp.swapaxes(jnp.take(pieces[0], kv_ids, axis=1), 0, 1)
    picked_values = jnp.swapaxes(jnp.take(pieces[1], kv_ids, axis=1), 0, 1)
    running = attend(running, query_block, picked_keys, picked_values, jnp.int32(0), False, limit)
    row_max, row_total, row_sum = running
    finished = (row_sum / row_total[:, :, None]).astype(jnp.bfloat16)
    finished = jnp.transpose(finished, (1, 0, 2))
    returned = lax.all_to_all(finished, "seq", split_axis=0, concat_axis=1, tiled=True)
    return returned.reshape(1, row_count, heads_here * head_size)


def solution(mesh):
    return jax.shard_map(
        body,
        mesh=mesh,
        in_specs=(
            P("section", "seq", "tensor"),
            P("section", "seq", "tensor"),
            P("section", "seq", "tensor"),
            P("section", "seq", "tensor"),
            P("section", "seq", "tensor"),
            P("section", "seq", "tensor"),
            P("section", "tensor", "seq", None),
            P("section", "tensor", "seq", None),
            P("section"),
        ),
        out_specs=P("section", "seq", "tensor"),
        check_vma=False,
    )
```

profile of v0, /device:TPU:0, one launch (start us, length us, event | category | flops | bytes accessed | tf_op | source)
XLA Modules:
  0.0 120.3 jit_solution(3274771388179172553)
XLA Ops:
  0.0 3.0 %collective-permute-start = (bf16[64,4096]{1,0:T(8,128)(2,1)}, bf16[64,4096]{1,0:T(8,128)(2,1)S(1)}, u32[]{:S(2)}, u32[]{:S(2)}) collective-permute-start(bf16[64,4096]{1,0:T(8,128)(2,1)} %bitcast.60), channel_id=1, source_target_pairs={{16,0},{0,16},{17,1},{1,17},{18,2},{2,18},{19,3},{3,19},{20,4},{4,... | collective-permute-start | bytes 1572872 | tf_op jit(solution)/shard_map/ppermute | solution.py:11
  3.0 0.8 convert_bitcast_fusion
  3.7 0.9 copy.39
  4.6 2.1 %collective-permute-start.2 = (bf16[64,256]{0,1:T(8,128)(2,1)S(1)}, bf16[64,256]{0,1:T(8,128)(2,1)S(1)}, u32[]{:S(2)}, u32[]{:S(2)}) collective-permute-start(bf16[64,256]{0,1:T(8,128)(2,1)S(1)} %bitcast.59), channel_id=1, source_target_pairs={{16,0},{0,16},{17,1},{1,17},{18,2},{2,18},{19,3},{3,19},{20,4},{4,... | collective-permute-start | bytes 98312 | tf_op jit(solution)/shard_map/ppermute | solution.py:11
  6.7 0.7 convert_bitcast_fusion.2
  7.4 0.9 copy.42
  8.3 2.1 %collective-permute-start.4 = (bf16[64,256]{0,1:T(8,128)(2,1)S(1)}, bf16[64,256]{0,1:T(8,128)(2,1)S(1)}, u32[]{:S(2)}, u32[]{:S(2)}) collective-permute-start(bf16[64,256]{0,1:T(8,128)(2,1)S(1)} %bitcast.58), channel_id=1, source_target_pairs={{16,0},{0,16},{17,1},{1,17},{18,2},{2,18},{19,3},{3,19},{20,4},{4,... | collective-permute-start | bytes 98312 | tf_op jit(solution)/shard_map/ppermute | solution.py:11
  10.4 0.7 convert_bitcast_fusion.1
  11.1 5.2 %collective-permute-done.1 = bf16[64,128]{1,0:T(8,128)(2,1)S(1)} collective-permute-done((bf16[64,128]{1,0:T(8,128)(2,1)S(1)}, bf16[64,128]{1,0:T(8,128)(2,1)S(1)}, u32[]{:S(2)}, u32[]{:S(2)}) %collective-permute-start.1) | collective-permute-done | bytes 16416 | tf_op jit(solution)/shard_map/ppermute | solution.py:11
  16.3 2.0 %collective-permute-start.5 = (bf16[64,8]{0,1:T(8,128)(2,1)S(1)}, bf16[64,8]{0,1:T(8,128)(2,1)S(1)}, u32[]{:S(2)}, u32[]{:S(2)}) collective-permute-start(bf16[64,8]{0,1:T(8,128)(2,1)S(1)} %convert_bitcast_fusion.1), channel_id=1, source_target_pairs={{16,0},{0,16},{17,1},{1,17},{18,2},{2,18},{19,3},{3,19},{20,4},{4,... | collective-permute-start | bytes 3080 | tf_op jit(solution)/shard_map/ppermute | solution.py:11
  19.2 1.1 copy.36
  20.3 4.9 %all-to-all-start = ((bf16[64,32,128]{2,0,1:T(8,128)(2,1)}), bf16[64,32,128]{2,0,1:T(8,128)(2,1)S(1)}, u32[]{:S(2)}, u32[]{:S(2)}) async-start(bf16[64,32,128]{2,0,1:T(8,128)(2,1)} %copy.36), calls=%async_computation | async-start | bytes 1048576 | tf_op jit(solution)/shard_map/all_to_all | solution.py:120
  25.2 19.9 %all-gather = bf16[1,2,512,128]{3,2,1,0:T(8,128)(2,1)S(1)} all-gather(bf16[1,2,128,128]{3,2,1,0:T(8,128)(2,1)S(1)} %copy-done.5), channel_id=2, replica_groups=mesh['section'=2,'seq'=4,'tensor'=4] {'seq'}, dimensions={2}, use_global_device_ids=true | all-gather | bytes 327680 | tf_op jit(solution)/shard_map/all_gather | solution.py:130
  45.2 13.9 %all-gather.1 = bf16[1,2,512,128]{3,2,1,0:T(8,128)(2,1)S(1)} all-gather(bf16[1,2,128,128]{3,2,1,0:T(8,128)(2,1)S(1)} %copy-done.6), channel_id=3, replica_groups=mesh['section'=2,'seq'=4,'tensor'=4] {'seq'}, dimensions={2}, use_global_device_ids=true | all-gather | bytes 327680 | tf_op jit(solution)/shard_map/all_gather | solution.py:131
  59.1 0.7 gather_fusion
  59.8 1.7 %gather_fusion.1 = bf16[8,512,128]{2,1,0:T(8,128)(2,1)} fusion(bf16[2,512,128]{2,1,0:T(8,128)(2,1)S(1)} %bitcast.50, s32[1024]{0:T(1024)S(1)} %pad_clamp_fusion), kind=kCustom, calls=%fused_computation.2.clone | custom fusion | bytes 2097184 | tf_op jit(solution)/shard_map/jit(_take)/gather | solution.py:137
  62.2 1.1 broadcast_in_dim.78
  63.4 13.6 %all_gather.14 = bf16[256,2,128]{2,0,1:T(8,128)(2,1)S(1)} all-gather(bf16[64,2,128]{2,0,1:T(8,128)(2,1)S(1)} %copy.41), channel_id=1, replica_groups=mesh['section'=2,'seq'=4,'tensor'=4] {'seq'}, dimensions={0}, use_global_device_ids=true | all-gather | bytes 163840 | tf_op jit(solution)/shard_map/all_gather | solution.py:143
  77.1 1.4 %gather_fusion.2 = bf16[8,256,128]{2,1,0:T(8,128)(2,1)} fusion(bf16[256,2,128]{2,0,1:T(8,128)(2,1)S(1)} %all_gather.14, s32[1024]{0:T(1024)S(1)} %pad_clamp_fusion), kind=kCustom, calls=%fused_computation.1.clone | custom fusion | bytes 1048608 | tf_op jit(solution)/shard_map/jit(_take)/gather | solution.py:146
  78.6 13.3 %all_gather.15 = bf16[256,2,128]{2,0,1:T(8,128)(2,1)S(1)} all-gather(bf16[64,2,128]{2,0,1:T(8,128)(2,1)S(1)} %copy.44), channel_id=1, replica_groups=mesh['section'=2,'seq'=4,'tensor'=4] {'seq'}, dimensions={0}, use_global_device_ids=true | all-gather | bytes 163840 | tf_op jit(solution)/shard_map/all_gather | solution.py:144
  92.0 1.4 %gather_fusion.3 = bf16[8,256,128]{2,1,0:T(8,128)(2,1)} fusion(bf16[256,2,128]{2,0,1:T(8,128)(2,1)S(1)} %all_gather.15, s32[1024]{0:T(1024)S(1)} %pad_clamp_fusion), kind=kCustom, calls=%fused_computation.3.clone | custom fusion | bytes 1048608 | tf_op jit(solution)/shard_map/jit(_take)/gather | solution.py:147
  93.4 1.6 %fusion.18 = (f32[8,256]{1,0:T(8,128)S(1)}, f32[8,256,256]{1,2,0:T(8,128)S(1)}) fusion(pred[256,256]{0,1:T(8,128)(4,1)S(1)} %iota_compare_fusion, bf16[8,256,128]{2,1,0:T(8,128)(2,1)S(1)} %bitcast.52, bf16[8,256,128]{2,1,0:T(8,128)(2,1)} %gather_fusion.2, pred[8]{0:T(512)(128)(4,1)S(1)} %compare_and_fusion), kind=kOutput, calls=%fused_computation.27 | convolution fusion | flops 136050688 | bytes 3219464 | tf_op jit(solution)/shard_map/while/body/eval_jaxpr/cond/branch_1_fun/hqd,hkd->hqk/dot_general | solution.py:36
  95.2 5.8 %conditional.1 = ((f32[8,256]{1,0:T(8,128)S(1)}, f32[8,256]{1,0:T(8,128)S(1)}, f32[8,256,128]{2,1,0:T(8,128)})) conditional(s32[]{:T(128)} %convert_element_type.63, (f32[8,256]{1,0:T(8,128)S(1)}, f32[8,256]{1,0:T(8,128)S(1)}, f32[8,256,128]{2,1,0:T(8,128)}) %tuple.27, (s32[]{:T(128)}, s32[512]{0:T(512)S(1)}, ...), branch_computations={%region_0.2_spmd, %region_1.5_spmd.clone} | conditional | flops 552079872 | bytes 32116872 | solution.py:76
  95.2 0.7 broadcast_compare_fusion
  95.8 0.9 fusion
  96.7 1.3 %fusion.2 = f32[8,256]{1,0:T(8,128)S(1)} fusion(f32[8,256,512]{2,1,0:T(8,128)S(1)} %get-tuple-element.183, f32[8,256]{1,0:T(8,128)S(1)} %max.10, pred[512]{0:T(512)(128)(4,1)S(1)} %broadcast_compare_fusion), kind=kLoop, calls=%fused_computation.8 | loop fusion | flops 5240832 | bytes 4211200 | tf_op jit(solution)/shard_map/while/body/eval_jaxpr/cond/branch_1_fun/reduce_sum | solution.py:57
  98.3 1.7 %fusion.6 = f32[8,256,128]{2,1,0:T(8,128)S(1)} fusion(f32[8,256,512]{2,1,0:T(8,128)S(1)} %get-tuple-element.183, f32[8,256]{1,0:T(8,128)S(1)} %max.10, pred[512]{0:T(512)(128)(4,1)S(1)} %broadcast_compare_fusion, bf16[8,512,128]{2,1,0:T(8,128)(2,1)S(1)} %copy-done, bf16[8,512,128]{2,1,0:T(8,128)(2,1)S(1)} %get-tuple-element.164, ...), kind=kOutput, calls=%fused_computation.11 | convolution fusion | flops 274726912 | bytes 8405512 | tf_op jit(solution)/shard_map/while/body/eval_jaxpr/cond/branch_1_fun/hqk,hkd->hqd/dot_general | solution.py:58
  100.0 1.0 copy-done.2
  101.5 0.7 copy-done.3
  102.3 1.4 %fusion.23 = bf16[256,8,128]{2,0,1:T(8,128)(2,1)S(1)} fusion(f32[8,256,256]{1,2,0:T(8,128)S(1)} %get-tuple-element.185, f32[8,256]{1,0:T(8,128)S(1)} %max.9, f32[8,256,128]{2,1,0:T(8,128)S(1)} %copy-done.3, pred[256,256]{0,1:T(8,128)(4,1)S(1)} %iota_compare_fusion, bf16[8,256,128]{2,1,0:T(8,128)(2,1)S(1)} %copy-done.4, ...), kind=kOutput, calls=%fused_computation.33 | convolution fusion | flops 138149888 | bytes 4284424 | tf_op jit(solution)/shard_map/while/body/eval_jaxpr/cond/branch_1_fun/hqk,hkd->hqd/dot_general | solution.py:58
  104.1 15.0 %all_to_all.33 = bf16[256,8,128]{2,1,0:T(8,128)(2,1)S(1)} all-to-all(bf16[256,8,128]{2,1,0:T(8,128)(2,1)S(1)} %copy.46), channel_id=1, replica_groups=mesh['section'=2,'seq'=4,'tensor'=4] {'seq'}, dimensions={0} | all-to-all | bytes 1048576 | tf_op jit(solution)/shard_map/all_to_all | solution.py:152
  119.3 1.0 reshape.69
  (47 shorter events, 2.7 us)
Async XLA Ops:
  0.0 18.4 %collective-permute-start = (bf16[64,4096]{1,0:T(8,128)(2,1)}, bf16[64,4096]{1,0:T(8,128)(2,1)S(1)}, u32[]{:S(2)}, u32[]{:S(2)}) collective-permute-start(bf16[64,4096]{1,0:T(8,128)(2,1)} %bitcast.60), channel_id=1, source_target_pairs={{16,0},{0,16},{17,1},{1,17},{18,2},{2,18},{19,3},{3,19},{20,4},{4,... | collective-permute-start | bytes 1572872 | tf_op jit(solution)/shard_map/ppermute | solution.py:11
  3.7 12.6 %collective-permute-start.1 = (bf16[64,128]{1,0:T(8,128)(2,1)S(1)}, bf16[64,128]{1,0:T(8,128)(2,1)S(1)}, u32[]{:S(2)}, u32[]{:S(2)}) collective-permute-start(bf16[64,128]{1,0:T(8,128)(2,1)S(1)} %convert_bitcast_fusion), channel_id=1, source_target_pairs={{16,0},{0,16},{17,1},{1,17},{18,2},{2,18},{19,3},{3,19},{20,4},{4,... | collective-permute-start | bytes 49160 | tf_op jit(solution)/shard_map/ppermute | solution.py:11
  4.6 58.7 %collective-permute-start.2 = (bf16[64,256]{0,1:T(8,128)(2,1)S(1)}, bf16[64,256]{0,1:T(8,128)(2,1)S(1)}, u32[]{:S(2)}, u32[]{:S(2)}) collective-permute-start(bf16[64,256]{0,1:T(8,128)(2,1)S(1)} %bitcast.59), channel_id=1, source_target_pairs={{16,0},{0,16},{17,1},{1,17},{18,2},{2,18},{19,3},{3,19},{20,4},{4,... | collective-permute-start | bytes 98312 | tf_op jit(solution)/shard_map/ppermute | solution.py:11
  7.4 55.9 %collective-permute-start.3 = (bf16[64,8]{0,1:T(8,128)(2,1)S(1)}, bf16[64,8]{0,1:T(8,128)(2,1)S(1)}, u32[]{:S(2)}, u32[]{:S(2)}) collective-permute-start(bf16[64,8]{0,1:T(8,128)(2,1)S(1)} %convert_bitcast_fusion.2), channel_id=1, source_target_pairs={{16,0},{0,16},{17,1},{1,17},{18,2},{2,18},{19,3},{3,19},{20,4},{4,... | collective-permute-start | bytes 3080 | tf_op jit(solution)/shard_map/ppermute | solution.py:11
  8.3 70.2 %collective-permute-start.4 = (bf16[64,256]{0,1:T(8,128)(2,1)S(1)}, bf16[64,256]{0,1:T(8,128)(2,1)S(1)}, u32[]{:S(2)}, u32[]{:S(2)}) collective-permute-start(bf16[64,256]{0,1:T(8,128)(2,1)S(1)} %bitcast.58), channel_id=1, source_target_pairs={{16,0},{0,16},{17,1},{1,17},{18,2},{2,18},{19,3},{3,19},{20,4},{4,... | collective-permute-start | bytes 98312 | tf_op jit(solution)/shard_map/ppermute | solution.py:11
  16.3 47.0 %collective-permute-start.5 = (bf16[64,8]{0,1:T(8,128)(2,1)S(1)}, bf16[64,8]{0,1:T(8,128)(2,1)S(1)}, u32[]{:S(2)}, u32[]{:S(2)}) collective-permute-start(bf16[64,8]{0,1:T(8,128)(2,1)S(1)} %convert_bitcast_fusion.1), channel_id=1, source_target_pairs={{16,0},{0,16},{17,1},{1,17},{18,2},{2,18},{19,3},{3,19},{20,4},{4,... | collective-permute-start | bytes 3080 | tf_op jit(solution)/shard_map/ppermute | solution.py:11
  18.9 6.2 %copy-start.5 = (bf16[1,2,128,128]{3,2,1,0:T(8,128)(2,1)S(1)}, bf16[1,2,128,128]{3,2,1,0:T(8,128)(2,1)}, u32[]{:S(2)}) copy-start(bf16[1,2,128,128]{3,2,1,0:T(8,128)(2,1)} %param.21) | copy-start | bytes 196612
  18.9 26.2 %copy-start.6 = (bf16[1,2,128,128]{3,2,1,0:T(8,128)(2,1)S(1)}, bf16[1,2,128,128]{3,2,1,0:T(8,128)(2,1)}, u32[]{:S(2)}) copy-start(bf16[1,2,128,128]{3,2,1,0:T(8,128)(2,1)} %param.22) | copy-start | bytes 196612
  20.3 73.1 %all-to-all-start = ((bf16[64,32,128]{2,0,1:T(8,128)(2,1)}), bf16[64,32,128]{2,0,1:T(8,128)(2,1)S(1)}, u32[]{:S(2)}, u32[]{:S(2)}) async-start(bf16[64,32,128]{2,0,1:T(8,128)(2,1)} %copy.36), calls=%async_computation | async-start | bytes 1048576 | tf_op jit(solution)/shard_map/all_to_all | solution.py:120
  96.7 1.3 %copy-start = (bf16[8,512,128]{2,1,0:T(8,128)(2,1)S(1)}, bf16[8,512,128]{2,1,0:T(8,128)(2,1)}, u32[]{:S(2)}) copy-start(bf16[8,512,128]{2,1,0:T(8,128)(2,1)} %get-tuple-element.165) | copy-start | bytes 3145732 | tf_op jit(solution)/shard_map/while/body/eval_jaxpr/cond
  96.7 1.5 %copy-start.1 = (f32[8,256,128]{2,1,0:T(8,128)S(1)}, f32[8,256,128]{2,1,0:T(8,128)}, u32[]{:S(2)}) copy-start(f32[8,256,128]{2,1,0:T(8,128)} %get-tuple-element.162) | copy-start | bytes 3145732 | tf_op jit(solution)/shard_map/while/body/eval_jaxpr/cond
  100.0 1.0 copy-start.2
  101.0 1.2 %copy-start.3 = (f32[8,256,128]{2,1,0:T(8,128)S(1)}, f32[8,256,128]{2,1,0:T(8,128)}, u32[]{:S(2)}) copy-start(f32[8,256,128]{2,1,0:T(8,128)} %get-tuple-element.147) | copy-start | bytes 3145732
  101.0 1.4 %copy-start.4 = (bf16[8,256,128]{2,1,0:T(8,128)(2,1)S(1)}, bf16[8,256,128]{2,1,0:T(8,128)(2,1)}, u32[]{:S(2)}) copy-start(bf16[8,256,128]{2,1,0:T(8,128)(2,1)} %gather_fusion.3) | copy-start | bytes 1572868
where the time goes:
time: 121 us; the launch traced here: 120 us
  blocking collectives  75.9 us (63%)
  starting transfers between devices  14 us (12%)
  local copies, waits for them, and re-layouts  13.7 us (11%)
  matrix products  5.59 us (5%)
  waiting for transfers between devices  5.23 us (4%)
  other arithmetic  4.94 us (4%)
    all_gather x1, blocking collectives, body(): lax.all_gather(cached_key_rows[0], 'seq', axis=1, tiled=True)  19.9 us
    all_to_all x1, blocking collectives, body(): lax.all_to_all(finished, 'seq', split_axis=0, concat_axis=1, tiled=True)  15 us
    all_gather x1, blocking collectives, body(): lax.all_gather(cached_value_rows[0], 'seq', axis=1, tiled=True)  13.9 us
    all_gather x1, blocking collectives, body(): lax.all_gather(section_key_rows, 'seq', axis=0, tiled=True)  13.6 us
    all_gather x1, blocking collectives, body(): lax.all_gather(section_value_rows, 'seq', axis=0, tiled=True)  13.3 us
    ppermute x6, starting transfers between devices, shifted(): return lax.ppermute(block, axis, route)  9.17 us
    ppermute x6, waiting for transfers between devices, shifted(): return lax.ppermute(block, axis, route)  5.23 us
    all_to_all x1, starting transfers between devices, body(): lax.all_to_all(queries, 'seq', split_axis=1, concat_axis=0, tiled=True)  4.87 us
  transfers between devices with their start and end apart: 7, of which 1 were waited for; matrix products, arithmetic and copies ran while one was open for 10% of the time, Pallas kernels for 0%

commit v1 on v0

--- a/solution.py
+++ b/solution.py
@@ -149,7 +149,19 @@
     row_max, row_total, row_sum = running
     finished = (row_sum / row_total[:, :, None]).astype(jnp.bfloat16)
     finished = jnp.transpose(finished, (1, 0, 2))
-    returned = lax.all_to_all(finished, "seq", split_axis=0, concat_axis=1, tiled=True)
+    ways, here = (lax.axis_size("seq"), lax.axis_index("seq"))
+    width = finished.shape[0] // ways
+    lengths = list(finished.shape)
+    lengths[0] = width
+    height = lengths[1]
+    lengths[1] = height * ways
+    full = jnp.zeros(lengths, finished.dtype)
+    for mask in range(ways):
+        part = lax.dynamic_slice_in_dim(finished, (here ^ mask) * width, width, axis=0)
+        if mask:
+            part = lax.ppermute(part, "seq", [(d, d ^ mask) for d in range(ways)])
+        full = lax.dynamic_update_slice_in_dim(full, part, (here ^ mask) * height, axis=1)
+    returned = full
     return returned.reshape(1, row_count, heads_here * head_size)
 
 

time: 121 us -> 108 us (0.89)
  blocking collectives: 75.9 us -> 59.6 us
  starting transfers between devices: 14 us -> 16.7 us
  local copies, waits for them, and re-layouts: 13.7 us -> 15.5 us
    all_to_all x1 -> x0, blocking collectives: 15 us -> none  [body(): lax.all_to_all(finished, 'seq', split_axis=0, concat_axis=1, tiled=True)]
    all_gather x1, blocking collectives: 19.9 us -> 14.4 us  [body(): lax.all_gather(cached_key_rows[0], 'seq', axis=1, tiled=True)]
    ppermute x6, waiting for transfers between devices: 5.23 us -> 0.02 us  [shifted(): return lax.ppermute(block, axis, route)]
    all_gather x1, blocking collectives: 13.9 us -> 18.4 us  [body(): lax.all_gather(cached_value_rows[0], 'seq', axis=1, tiled=True)]
    ppermute x0 -> x3, starting transfers between devices: none -> 4.45 us  [body(): part = lax.ppermute(part, 'seq', [(d, d ^ mask) for d in range(ways)])]
    ppermute x0 -> x3, waiting for transfers between devices: none -> 4.32 us  [body(): part = lax.ppermute(part, 'seq', [(d, d ^ mask) for d in range(ways)])]
    ppermute x6, starting transfers between devices: 9.17 us -> 7.69 us  [shifted(): return lax.ppermute(block, axis, route)]
    dynamic_update_slice x0 -> x5, local copies, waits for them, and re-layouts: none -> 1.43 us  [body(): lax.dynamic_update_slice_in_dim(full, part, (here ^ mask) * height, axis=1)]
  transfers between devices with their start and end apart: 7 -> 10, of which waited for: 1 -> 2; matrix products, arithmetic and copies ran while one was open for 10% -> 13% of each run, Pallas kernels for 0% -> 0%
where the time goes in v1:
time: 108 us
  blocking collectives  59.6 us (55%)
  starting transfers between devices  16.7 us (15%)
  local copies, waits for them, and re-layouts  15.5 us (14%)
  matrix products  5.6 us (5%)
  other arithmetic  4.93 us (5%)
  waiting for transfers between devices  4.34 us (4%)
    all_gather x1, blocking collectives, body(): lax.all_gather(cached_value_rows[0], 'seq', axis=1, tiled=True)  18.4 us
    all_gather x1, blocking collectives, body(): lax.all_gather(cached_key_rows[0], 'seq', axis=1, tiled=True)  14.4 us
    all_gather x1, blocking collectives, body(): lax.all_gather(section_key_rows, 'seq', axis=0, tiled=True)  13.3 us
    all_gather x1, blocking collectives, body(): lax.all_gather(section_value_rows, 'seq', axis=0, tiled=True)  13.3 us
    ppermute x6, starting transfers between devices, shifted(): return lax.ppermute(block, axis, route)  7.69 us
    all_to_all x1, starting transfers between devices, body(): lax.all_to_all(queries, 'seq', split_axis=1, concat_axis=0, tiled=True)  4.52 us
    ppermute x3, starting transfers between devices, body(): part = lax.ppermute(part, 'seq', [(d, d ^ mask) for d in range(ways)])  4.45 us
    ppermute x3, waiting for transfers between devices, body(): part = lax.ppermute(part, 'seq', [(d, d ^ mask) for d in range(ways)])  4.32 us
  transfers between devices with their start and end apart: 10, of which 2 were waited for; matrix products, arithmetic and copies ran while one was open for 13% of the time, Pallas kernels for 0%

profile of v1, /device:TPU:0, one launch (start us, length us, event | category | flops | bytes accessed | tf_op | source)
XLA Modules:
  0.0 107.6 jit_solution(7129141240492421645)
XLA Ops:
  0.0 3.0 %collective-permute-start = (bf16[64,4096]{1,0:T(8,128)(2,1)}, bf16[64,4096]{1,0:T(8,128)(2,1)S(1)}, u32[]{:S(2)}, u32[]{:S(2)}) collective-permute-start(bf16[64,4096]{1,0:T(8,128)(2,1)} %bitcast.60), channel_id=1, source_target_pairs={{16,0},{0,16},{17,1},{1,17},{18,2},{2,18},{19,3},{3,19},{20,4},{4,... | collective-permute-start | bytes 1572872 | tf_op jit(solution)/shard_map/ppermute | solution.py:11
  3.0 0.8 convert_bitcast_fusion
  3.7 0.9 copy.42
  4.6 2.1 %collective-permute-start.2 = (bf16[64,256]{0,1:T(8,128)(2,1)S(1)}, bf16[64,256]{0,1:T(8,128)(2,1)S(1)}, u32[]{:S(2)}, u32[]{:S(2)}) collective-permute-start(bf16[64,256]{0,1:T(8,128)(2,1)S(1)} %bitcast.59), channel_id=1, source_target_pairs={{16,0},{0,16},{17,1},{1,17},{18,2},{2,18},{19,3},{3,19},{20,4},{4,... | collective-permute-start | bytes 98312 | tf_op jit(solution)/shard_map/ppermute | solution.py:11
  7.4 0.9 copy.45
  8.3 2.1 %collective-permute-start.4 = (bf16[64,256]{0,1:T(8,128)(2,1)S(1)}, bf16[64,256]{0,1:T(8,128)(2,1)S(1)}, u32[]{:S(2)}, u32[]{:S(2)}) collective-permute-start(bf16[64,256]{0,1:T(8,128)(2,1)S(1)} %bitcast.58), channel_id=1, source_target_pairs={{16,0},{0,16},{17,1},{1,17},{18,2},{2,18},{19,3},{3,19},{20,4},{4,... | collective-permute-start | bytes 98312 | tf_op jit(solution)/shard_map/ppermute | solution.py:11
  11.1 14.4 %all-gather = bf16[1,2,512,128]{3,2,1,0:T(8,128)(2,1)S(1)} all-gather(bf16[1,2,128,128]{3,2,1,0:T(8,128)(2,1)} %param.21), channel_id=2, replica_groups=mesh['section'=2,'seq'=4,'tensor'=4] {'seq'}, dimensions={2}, use_global_device_ids=true | all-gather | bytes 327680 | tf_op jit(solution)/shard_map/all_gather | solution.py:130
  26.9 1.1 %copy.39 = bf16[64,32,128]{2,0,1:T(8,128)(2,1)} copy(bf16[64,32,128]{0,2,1:T(8,128)(2,1)S(1)} %bitcast.52) | data formatting | bytes 1048576 | tf_op jit(solution)/shard_map/reshape | solution.py:107
  28.0 4.5 %all-to-all-start = ((bf16[64,32,128]{2,0,1:T(8,128)(2,1)}), bf16[64,32,128]{2,0,1:T(8,128)(2,1)S(1)}, u32[]{:S(2)}, u32[]{:S(2)}) async-start(bf16[64,32,128]{2,0,1:T(8,128)(2,1)} %copy.39), calls=%async_computation | async-start | bytes 1048576 | tf_op jit(solution)/shard_map/all_to_all | solution.py:120
  32.5 18.4 %all-gather.1 = bf16[1,2,512,128]{3,2,1,0:T(8,128)(2,1)S(1)} all-gather(bf16[1,2,128,128]{3,2,1,0:T(8,128)(2,1)S(1)} %copy-done.6), channel_id=3, replica_groups=mesh['section'=2,'seq'=4,'tensor'=4] {'seq'}, dimensions={2}, use_global_device_ids=true | all-gather | bytes 327680 | tf_op jit(solution)/shard_map/all_gather | solution.py:131
  51.0 0.7 gather_fusion
  51.8 1.7 %gather_fusion.1 = bf16[8,512,128]{2,1,0:T(8,128)(2,1)} fusion(bf16[2,512,128]{2,1,0:T(8,128)(2,1)S(1)} %bitcast.51, s32[1024]{0:T(1024)S(1)} %pad_clamp_fusion), kind=kCustom, calls=%fused_computation.2.clone | custom fusion | bytes 2097184 | tf_op jit(solution)/shard_map/jit(_take)/gather | solution.py:137
  54.1 1.1 %broadcast_in_dim.82 = f32[8,256,128]{2,1,0:T(8,128)} broadcast(f32[]{:T(128)} %constant.70.clone.1), dimensions={} | broadcast | bytes 1048580 | tf_op jit(solution)/shard_map/broadcast_in_dim | solution.py:125
  55.4 13.3 %all_gather.14 = bf16[256,2,128]{2,0,1:T(8,128)(2,1)S(1)} all-gather(bf16[64,2,128]{2,0,1:T(8,128)(2,1)S(1)} %copy.44), channel_id=1, replica_groups=mesh['section'=2,'seq'=4,'tensor'=4] {'seq'}, dimensions={0}, use_global_device_ids=true | all-gather | bytes 163840 | tf_op jit(solution)/shard_map/all_gather | solution.py:143
  68.7 1.4 %gather_fusion.2 = bf16[8,256,128]{2,1,0:T(8,128)(2,1)} fusion(bf16[256,2,128]{2,0,1:T(8,128)(2,1)S(1)} %all_gather.14, s32[1024]{0:T(1024)S(1)} %pad_clamp_fusion), kind=kCustom, calls=%fused_computation.1.clone | custom fusion | bytes 1048608 | tf_op jit(solution)/shard_map/jit(_take)/gather | solution.py:146
  70.3 13.3 %all_gather.15 = bf16[256,2,128]{2,0,1:T(8,128)(2,1)S(1)} all-gather(bf16[64,2,128]{2,0,1:T(8,128)(2,1)S(1)} %copy.47), channel_id=1, replica_groups=mesh['section'=2,'seq'=4,'tensor'=4] {'seq'}, dimensions={0}, use_global_device_ids=true | all-gather | bytes 163840 | tf_op jit(solution)/shard_map/all_gather | solution.py:144
  83.6 1.4 %gather_fusion.3 = bf16[8,256,128]{2,1,0:T(8,128)(2,1)} fusion(bf16[256,2,128]{2,0,1:T(8,128)(2,1)S(1)} %all_gather.15, s32[1024]{0:T(1024)S(1)} %pad_clamp_fusion), kind=kCustom, calls=%fused_computation.3.clone | custom fusion | bytes 1048608 | tf_op jit(solution)/shard_map/jit(_take)/gather | solution.py:147
  85.1 1.6 %fusion.18 = (f32[8,256]{1,0:T(8,128)S(1)}, f32[8,256,256]{1,2,0:T(8,128)S(1)}) fusion(pred[256,256]{0,1:T(8,128)(4,1)S(1)} %iota_compare_fusion, bf16[8,256,128]{2,1,0:T(8,128)(2,1)S(1)} %bitcast.53, bf16[8,256,128]{2,1,0:T(8,128)(2,1)} %gather_fusion.2, pred[8]{0:T(512)(128)(4,1)S(1)} %compare_and_fusion), kind=kOutput, calls=%fused_computation.27 | convolution fusion | flops 136050688 | bytes 3219464 | tf_op jit(solution)/shard_map/while/body/eval_jaxpr/cond/branch_1_fun/hqd,hkd->hqk/dot_general | solution.py:36
  86.8 5.8 %conditional.1 = ((f32[8,256]{1,0:T(8,128)S(1)}, f32[8,256]{1,0:T(8,128)S(1)}, f32[8,256,128]{2,1,0:T(8,128)})) conditional(s32[]{:T(128)} %convert_element_type.63, (f32[8,256]{1,0:T(8,128)S(1)}, f32[8,256]{1,0:T(8,128)S(1)}, f32[8,256,128]{2,1,0:T(8,128)}) %tuple.27, (s32[]{:T(128)}, s32[512]{0:T(512)S(1)}, ...), branch_computations={%region_0.2_spmd, %region_1.5_spmd.clone} | conditional | flops 552079872 | bytes 32116872 | solution.py:76
  87.5 0.9 fusion
  88.4 1.3 %fusion.2 = f32[8,256]{1,0:T(8,128)S(1)} fusion(f32[8,256,512]{2,1,0:T(8,128)S(1)} %get-tuple-element.183, f32[8,256]{1,0:T(8,128)S(1)} %max.10, pred[512]{0:T(512)(128)(4,1)S(1)} %broadcast_compare_fusion), kind=kLoop, calls=%fused_computation.8 | loop fusion | flops 5240832 | bytes 4211200 | tf_op jit(solution)/shard_map/while/body/eval_jaxpr/cond/branch_1_fun/reduce_sum | solution.py:57
  89.9 1.7 %fusion.6 = f32[8,256,128]{2,1,0:T(8,128)S(1)} fusion(f32[8,256,512]{2,1,0:T(8,128)S(1)} %get-tuple-element.183, f32[8,256]{1,0:T(8,128)S(1)} %max.10, pred[512]{0:T(512)(128)(4,1)S(1)} %broadcast_compare_fusion, bf16[8,512,128]{2,1,0:T(8,128)(2,1)S(1)} %copy-done, bf16[8,512,128]{2,1,0:T(8,128)(2,1)S(1)} %get-tuple-element.164, ...), kind=kOutput, calls=%fused_computation.11 | convolution fusion | flops 274726912 | bytes 8405512 | tf_op jit(solution)/shard_map/while/body/eval_jaxpr/cond/branch_1_fun/hqk,hkd->hqd/dot_general | solution.py:58
  91.6 1.0 copy-done.2
  94.0 1.4 %fusion.22 = bf16[8,256,128]{2,1,0:T(8,128)(2,1)S(1)} fusion(f32[8,256,256]{1,2,0:T(8,128)S(1)} %get-tuple-element.188, f32[8,256]{1,0:T(8,128)S(1)} %max.9, f32[8,256,128]{2,1,0:T(8,128)S(1)} %copy-done.3, pred[256,256]{0,1:T(8,128)(4,1)S(1)} %iota_compare_fusion, bf16[8,256,128]{2,1,0:T(8,128)(2,1)S(1)} %copy-done.5, ...), kind=kOutput, calls=%fused_computation.32 | convolution fusion | flops 138149888 | bytes 4284424 | tf_op jit(solution)/shard_map/while/body/eval_jaxpr/cond/branch_1_fun/hqk,hkd->hqd/dot_general | solution.py:58
  95.4 0.8 copy-done.4
  96.3 1.0 collective-permute-start.6
  97.2 2.4 %collective-permute-start.7 = (bf16[64,8,128]{2,0,1:T(8,128)(2,1)S(1)}, bf16[64,8,128]{2,0,1:T(8,128)(2,1)S(1)}, u32[]{:S(2)}, u32[]{:S(2)}) collective-permute-start(bf16[64,8,128]{2,0,1:T(8,128)(2,1)S(1)} %get-tuple-element.185), channel_id=1, source_target_pairs={{0,8},{4,12},{8,0},{12,4},{1,9},{5,13},{9,1},{13,5},{2,10},{6,14},... | collective-permute-start | bytes 393224 | tf_op jit(solution)/shard_map/ppermute | solution.py:162
  99.6 1.1 %collective-permute-start.8 = (bf16[64,8,128]{2,0,1:T(8,128)(2,1)S(1)}, bf16[64,8,128]{2,0,1:T(8,128)(2,1)S(1)}, u32[]{:S(2)}, u32[]{:S(2)}) collective-permute-start(bf16[64,8,128]{2,0,1:T(8,128)(2,1)S(1)} %get-tuple-element.184), channel_id=1, source_target_pairs={{0,12},{4,8},{8,4},{12,0},{1,13},{5,9},{9,5},{13,1},{2,14},{6,10},... | collective-permute-start | bytes 393224 | tf_op jit(solution)/shard_map/ppermute | solution.py:162
  100.8 0.9 bitcast_dynamic-update-slice_fusion
  101.8 2.7 %collective-permute-done.7 = bf16[64,8,128]{2,0,1:T(8,128)(2,1)S(1)} collective-permute-done((bf16[64,8,128]{2,0,1:T(8,128)(2,1)S(1)}, bf16[64,8,128]{2,0,1:T(8,128)(2,1)S(1)}, u32[]{:S(2)}, u32[]{:S(2)}) %collective-permute-start.7) | collective-permute-done | bytes 131104 | tf_op jit(solution)/shard_map/ppermute | solution.py:162
  104.9 1.6 %collective-permute-done.8 = bf16[64,8,128]{2,0,1:T(8,128)(2,1)S(1)} collective-permute-done((bf16[64,8,128]{2,0,1:T(8,128)(2,1)S(1)}, bf16[64,8,128]{2,0,1:T(8,128)(2,1)S(1)}, u32[]{:S(2)}, u32[]{:S(2)}) %collective-permute-start.8) | collective-permute-done | bytes 131104 | tf_op jit(solution)/shard_map/ppermute | solution.py:162
  106.6 1.0 reshape.68
  (57 shorter events, 6.1 us)
Async XLA Ops:
  0.0 26.2 %collective-permute-start = (bf16[64,4096]{1,0:T(8,128)(2,1)}, bf16[64,4096]{1,0:T(8,128)(2,1)S(1)}, u32[]{:S(2)}, u32[]{:S(2)}) collective-permute-start(bf16[64,4096]{1,0:T(8,128)(2,1)} %bitcast.60), channel_id=1, source_target_pairs={{16,0},{0,16},{17,1},{1,17},{18,2},{2,18},{19,3},{3,19},{20,4},{4,... | collective-permute-start | bytes 1572872 | tf_op jit(solution)/shard_map/ppermute | solution.py:11
  3.7 21.8 %collective-permute-start.1 = (bf16[64,128]{1,0:T(8,128)(2,1)S(1)}, bf16[64,128]{1,0:T(8,128)(2,1)S(1)}, u32[]{:S(2)}, u32[]{:S(2)}) collective-permute-start(bf16[64,128]{1,0:T(8,128)(2,1)S(1)} %convert_bitcast_fusion), channel_id=1, source_target_pairs={{16,0},{0,16},{17,1},{1,17},{18,2},{2,18},{19,3},{3,19},{20,4},{4,... | collective-permute-start | bytes 49160 | tf_op jit(solution)/shard_map/ppermute | solution.py:11
  4.6 50.6 %collective-permute-start.2 = (bf16[64,256]{0,1:T(8,128)(2,1)S(1)}, bf16[64,256]{0,1:T(8,128)(2,1)S(1)}, u32[]{:S(2)}, u32[]{:S(2)}) collective-permute-start(bf16[64,256]{0,1:T(8,128)(2,1)S(1)} %bitcast.59), channel_id=1, source_target_pairs={{16,0},{0,16},{17,1},{1,17},{18,2},{2,18},{19,3},{3,19},{20,4},{4,... | collective-permute-start | bytes 98312 | tf_op jit(solution)/shard_map/ppermute | solution.py:11
  7.4 47.8 %collective-permute-start.3 = (bf16[64,8]{0,1:T(8,128)(2,1)S(1)}, bf16[64,8]{0,1:T(8,128)(2,1)S(1)}, u32[]{:S(2)}, u32[]{:S(2)}) collective-permute-start(bf16[64,8]{0,1:T(8,128)(2,1)S(1)} %convert_bitcast_fusion.2), channel_id=1, source_target_pairs={{16,0},{0,16},{17,1},{1,17},{18,2},{2,18},{19,3},{3,19},{20,4},{4,... | collective-permute-start | bytes 3080 | tf_op jit(solution)/shard_map/ppermute | solution.py:11
  8.3 61.9 %collective-permute-start.4 = (bf16[64,256]{0,1:T(8,128)(2,1)S(1)}, bf16[64,256]{0,1:T(8,128)(2,1)S(1)}, u32[]{:S(2)}, u32[]{:S(2)}) collective-permute-start(bf16[64,256]{0,1:T(8,128)(2,1)S(1)} %bitcast.58), channel_id=1, source_target_pairs={{16,0},{0,16},{17,1},{1,17},{18,2},{2,18},{19,3},{3,19},{20,4},{4,... | collective-permute-start | bytes 98312 | tf_op jit(solution)/shard_map/ppermute | solution.py:11
  25.5 29.7 %collective-permute-start.5 = (bf16[64,8]{0,1:T(8,128)(2,1)S(1)}, bf16[64,8]{0,1:T(8,128)(2,1)S(1)}, u32[]{:S(2)}, u32[]{:S(2)}) collective-permute-start(bf16[64,8]{0,1:T(8,128)(2,1)S(1)} %convert_bitcast_fusion.1), channel_id=1, source_target_pairs={{16,0},{0,16},{17,1},{1,17},{18,2},{2,18},{19,3},{3,19},{20,4},{4,... | collective-permute-start | bytes 3080 | tf_op jit(solution)/shard_map/ppermute | solution.py:11
  26.7 5.9 %copy-start.6 = (bf16[1,2,128,128]{3,2,1,0:T(8,128)(2,1)S(1)}, bf16[1,2,128,128]{3,2,1,0:T(8,128)(2,1)}, u32[]{:S(2)}) copy-start(bf16[1,2,128,128]{3,2,1,0:T(8,128)(2,1)} %param.22) | copy-start | bytes 196612
  28.0 57.0 %all-to-all-start = ((bf16[64,32,128]{2,0,1:T(8,128)(2,1)}), bf16[64,32,128]{2,0,1:T(8,128)(2,1)S(1)}, u32[]{:S(2)}, u32[]{:S(2)}) async-start(bf16[64,32,128]{2,0,1:T(8,128)(2,1)} %copy.39), calls=%async_computation | async-start | bytes 1048576 | tf_op jit(solution)/shard_map/all_to_all | solution.py:120
  88.4 1.3 %copy-start = (bf16[8,512,128]{2,1,0:T(8,128)(2,1)S(1)}, bf16[8,512,128]{2,1,0:T(8,128)(2,1)}, u32[]{:S(2)}) copy-start(bf16[8,512,128]{2,1,0:T(8,128)(2,1)} %get-tuple-element.165) | copy-start | bytes 3145732 | tf_op jit(solution)/shard_map/while/body/eval_jaxpr/cond
  88.4 1.5 %copy-start.1 = (f32[8,256,128]{2,1,0:T(8,128)S(1)}, f32[8,256,128]{2,1,0:T(8,128)}, u32[]{:S(2)}) copy-start(f32[8,256,128]{2,1,0:T(8,128)} %get-tuple-element.162) | copy-start | bytes 3145732 | tf_op jit(solution)/shard_map/while/body/eval_jaxpr/cond
  91.6 1.0 copy-start.2
  92.6 1.2 %copy-start.3 = (f32[8,256,128]{2,1,0:T(8,128)S(1)}, f32[8,256,128]{2,1,0:T(8,128)}, u32[]{:S(2)}) copy-start(f32[8,256,128]{2,1,0:T(8,128)} %get-tuple-element.147) | copy-start | bytes 3145732
  92.6 1.4 %copy-start.5 = (bf16[8,256,128]{2,1,0:T(8,128)(2,1)S(1)}, bf16[8,256,128]{2,1,0:T(8,128)(2,1)}, u32[]{:S(2)}) copy-start(bf16[8,256,128]{2,1,0:T(8,128)(2,1)} %gather_fusion.3) | copy-start | bytes 1572868
  95.4 0.8 copy-start.4
  96.3 5.5 %collective-permute-start.6 = (bf16[64,8,128]{2,0,1:T(8,128)(2,1)S(1)}, bf16[64,8,128]{2,0,1:T(8,128)(2,1)S(1)}, u32[]{:S(2)}, u32[]{:S(2)}) collective-permute-start(bf16[64,8,128]{2,0,1:T(8,128)(2,1)S(1)} %get-tuple-element.186), channel_id=1, source_target_pairs={{0,4},{4,0},{8,12},{12,8},{1,5},{5,1},{9,13},{13,9},{2,6},{6,2},{1... | collective-permute-start | bytes 393224 | tf_op jit(solution)/shard_map/ppermute | solution.py:162
  97.2 7.3 %collective-permute-start.7 = (bf16[64,8,128]{2,0,1:T(8,128)(2,1)S(1)}, bf16[64,8,128]{2,0,1:T(8,128)(2,1)S(1)}, u32[]{:S(2)}, u32[]{:S(2)}) collective-permute-start(bf16[64,8,128]{2,0,1:T(8,128)(2,1)S(1)} %get-tuple-element.185), channel_id=1, source_target_pairs={{0,8},{4,12},{8,0},{12,4},{1,9},{5,13},{9,1},{13,5},{2,10},{6,14},... | collective-permute-start | bytes 393224 | tf_op jit(solution)/shard_map/ppermute | solution.py:162
  99.6 6.9 %collective-permute-start.8 = (bf16[64,8,128]{2,0,1:T(8,128)(2,1)S(1)}, bf16[64,8,128]{2,0,1:T(8,128)(2,1)S(1)}, u32[]{:S(2)}, u32[]{:S(2)}) collective-permute-start(bf16[64,8,128]{2,0,1:T(8,128)(2,1)S(1)} %get-tuple-element.184), channel_id=1, source_target_pairs={{0,12},{4,8},{8,4},{12,0},{1,13},{5,9},{9,5},{13,1},{2,14},{6,10},... | collective-permute-start | bytes 393224 | tf_op jit(solution)/shard_map/ppermute | solution.py:162
